TPU v7x, 32 devices: a whole 2x2x4 slice. The times are simulated.
32 devices in a mesh: row: 2 (over core), col: 4 (over z), ind: 4 (over y, x).
Axes of the slice: x: 2, y: 2, z: 4, core: 2. Of those that a mesh axis runs over, the one named last changes fastest.
Arguments:
- dosages: bfloat16 [4096, 1024], P('ind', ('row', 'col'))
- annotations: bfloat16 [1024, 1024], P('ind', ('row', 'col')), may hold values from -6 to 6
- window_end: int32 [1024], P(('row', 'col')), may hold values from 512 to 1024, as said below
Outputs:
- ld_scores: float32 [1024, 1024], P('ind', ('row', 'col'))
Inputs may be any that keep to these rules, and one draw needn't show every extreme that they name: window_end is nondecreasing, window_end[j] > j, and window_end[j] <= min(1024, (j // 128 + 4) * 128), the last bound reached in every draw.
All inputs are finite; a program needn't handle non-finite values.
Results may differ from a plain program's by a relative error of at most 0.0029.
Values may be sent and summed in bfloat16 or wider, within the bound.
A program may use at most 64 MiB of HBM per device.

v0:
```python
import jax
import jax.numpy as jnp
from jax import lax
from jax.sharding import PartitionSpec as P


def from_behind(array, axis, by):
    count = lax.axis_size(axis)
    pairs = [(i, i + by) for i in range(count) if 0 <= i + by < count]
    return lax.ppermute(array, axis, pairs)


def per_device(dosages, annotations, window_end):
    band_count = lax.axis_size("col")
    column_index = lax.axis_index("col")
    tile_size = dosages.shape[1]
    ind_rows = dosages.shape[0]
    ann_rows = annotations.shape[0]
    group_width = band_count * tile_size
    sample_count = ind_rows * lax.axis_size("ind")
    window_ends = lax.all_gather(window_end, "col", axis=0, tiled=True)
    group_x, group_a = (
        lax.all_gather(dosages, "col", axis=1, tiled=True),
        lax.all_gather(annotations, "col", axis=1, tiled=True),
    )
    next_x, next_a = from_behind((group_x, group_a), "row", -1)
    wide_x = jnp.concatenate([group_x, next_x], axis=1)
    wide_a = jnp.concatenate([group_a, next_a], axis=1)
    band_x = lax.dynamic_slice_in_dim(wide_x, column_index * tile_size, group_width, 1)
    band_a = lax.dynamic_slice_in_dim(wide_a, column_index * tile_size, group_width, 1)
    rows_x = group_x.reshape(ind_rows, band_count, tile_size)
    cols_x = band_x.reshape(ind_rows, band_count, tile_size)
    partial_gram = jnp.einsum("inb,ine->nbe", rows_x, cols_x, preferred_element_type=jnp.float32)
    gram = lax.psum(partial_gram, "ind")
    correlation_matrix = gram / sample_count
    raw_rsquared = correlation_matrix * correlation_matrix
    unbiased_rsquared = raw_rsquared - (1.0 - raw_rsquared) / (sample_count - 2)
    group_start = lax.axis_index("row") * group_width
    block_ids = jnp.arange(band_count, dtype=jnp.int32)[:, None, None]
    within_window = jnp.arange(tile_size, dtype=jnp.int32)
    row_pos = group_start + block_ids * tile_size + within_window[None, :, None]
    col_pos = group_start + (block_ids + column_index) * tile_size + within_window[None, None, :]
    limit = window_ends.reshape(band_count, tile_size)[:, :, None]
    inside = col_pos < limit
    upper = jnp.where((col_pos >= row_pos) & inside, unbiased_rsquared, 0.0).astype(jnp.bfloat16)
    strict = jnp.where((col_pos > row_pos) & inside, unbiased_rsquared, 0.0).astype(jnp.bfloat16)
    annotation_rows = group_a.reshape(ann_rows, band_count, tile_size)
    cols_a = band_a.reshape(ann_rows, band_count, tile_size)
    direct = jnp.einsum("cne,nae->cna", cols_a, upper, preferred_element_type=jnp.float32)
    mirror = jnp.einsum("cna,nae->cne", annotation_rows, strict, preferred_element_type=jnp.float32)
    direct = direct.reshape(ann_rows, group_width)
    mirror = mirror.reshape(ann_rows, group_width)
    window_acc = jnp.zeros((ann_rows, 2 * group_width), jnp.float32)
    window_acc = lax.dynamic_update_slice_in_dim(window_acc, mirror, column_index * tile_size, 1)
    window_acc = window_acc.at[:, :group_width].add(direct)
    incoming = from_behind(window_acc[:, group_width:], "row", 1)
    combined = window_acc[:, :group_width] + incoming
    ld_scores = lax.psum_scatter(combined, "col", scatter_dimension=1, tiled=True)
    return ld_scores


def solution(mesh):
    in_specs = (P("ind", ("row", "col")), P("ind", ("row", "col")), P(("row", "col")))
    out_specs = P("ind", ("row", "col"))
    return jax.shard_map(
        per_device, mesh=mesh, in_specs=in_specs, out_specs=out_specs, check_vma=False
    )
```

profile of v0, /device:TPU:0, one launch (start us, length us, event | category | flops | bytes accessed | tf_op | source)
XLA Modules:
  0.0 139.3 jit_solution(7500563988074717324)
XLA Ops:
  6.5 1.8 %copy.16 = bf16[1024,128]{0,1:T(8,128)(2,1)} copy(bf16[1024,128]{1,0:T(8,128)(2,1)} %param.5) | data formatting | bytes 524288 | tf_op args[0]
  8.3 0.0 all-gather.3.cloned.1.call-update
  8.4 0.0 all-reduce.2.cloned.1.call-start
  8.4 31.2 %all-gather.3.cloned.1.call-done = bf16[1024,512]{0,1:T(8,128)(2,1)} async-done(((bf16[1024,128]{0,1:T(8,128)(2,1)}), bf16[1024,512]{0,1:T(8,128)(2,1)}) %all-gather.3.cloned.1.call-update) | async-done | bytes 1048592 | tf_op jit(solution)/shard_map/all_gather | solution.py:23
  39.6 1.3 collective-permute-start
  40.9 0.9 copy.18
  41.9 14.4 %all_gather.11 = bf16[256,512]{0,1:T(8,128)(2,1)S(1)} all-gather(bf16[256,128]{0,1:T(8,128)(2,1)S(1)} %copy.18), channel_id=1, replica_groups=mesh['row'=2,'col'=4,'ind'=4] {'col'}, dimensions={1}, use_global_device_ids=true | all-gather | bytes 327680 | tf_op jit(solution)/shard_map/all_gather | solution.py:24
  56.2 1.3 collective-permute-start.1
  57.6 0.0 collective-permute-done
  57.6 2.3 %fusion = bf16[1024,512]{0,1:T(8,128)(2,1)S(1)} fusion(s32[]{:T(128)S(6)} %select_n.12, bf16[1024,512]{0,1:T(8,128)(2,1)} %all-gather.3.cloned.1.call-done, bf16[1024,512]{0,1:T(8,128)(2,1)S(1)} %collective-permute-done), kind=kLoop, calls=%fused_computation.3 | loop fusion | flops 2097152 | bytes 3145732 | tf_op jit(solution)/shard_map/concatenate | solution.py:27
  59.9 0.0 copy-start.2
  59.9 1.1 convolution_bitcast_fusion
  61.0 0.0 all-reduce.2.cloned.1.call-update
  61.1 0.0 reduce-scatter.2.cloned.1.call-start
  61.1 0.1 iota_add_fusion
  61.2 9.1 %all-gather = s32[4,1,128]{2,1,0:T(1,128)S(1)} all-gather(s32[1,1,128]{2,1,0:T(1,128)S(1)} %bitcast.26), channel_id=1, replica_groups=mesh['row'=2,'col'=4,'ind'=4] {'col'}, dimensions={0}, use_global_device_ids=true | all-gather | bytes 2560 | tf_op jit(solution)/shard_map/all_gather | solution.py:21
  70.3 0.1 iota_add_fusion.1
  70.3 33.8 %all-reduce.2.cloned.1.call-done = f32[4,128,128]{1,2,0:T(8,128)} async-done(((f32[4,128,128]{1,2,0:T(8,128)}), f32[4,128,128]{1,2,0:T(8,128)}) %all-reduce.2.cloned.1.call-update) | async-done | bytes 262160 | tf_op jit(solution)/shard_map/psum | solution.py:34
  104.2 1.2 fusion.3
  105.4 0.2 copy.20
  105.6 0.1 broadcast_in_dim.11
  105.7 0.1 constant_dynamic-update-slice_fusion
  105.8 1.5 %collective-permute-start.2 = (f32[256,512]{1,0:T(8,128)S(1)}, f32[256,512]{1,0:T(8,128)S(1)}, u32[]{:S(2)}, u32[]{:S(2)}) collective-permute-start(f32[256,512]{1,0:T(8,128)S(1)} %slice.29), channel_id=1, source_target_pairs={{0,16},{1,17},{2,18},{3,19},{4,20},{5,21},{6,22},{7,23},{8,24},{9,... | collective-permute-start | bytes 1572872 | tf_op jit(solution)/shard_map/ppermute | solution.py:10
  107.3 0.6 compare_reduce_fusion
  107.9 0.0 collective-permute-done.1
  107.9 0.6 fusion.2
  108.6 0.4 fusion.4
  108.9 0.2 copy.23
  109.1 0.0 collective-permute-done.2
  109.1 1.6 %fusion.1 = f32[256,512]{1,0:T(8,128)} fusion(f32[256,512]{1,0:T(8,128)S(1)} %collective-permute-done.2, f32[256,512]{1,0:T(8,128)S(1)} %copy.23, f32[256,1024]{1,0:T(8,128)S(1)} %constant_dynamic-update-slice_fusion, pred[]{:T(512)} %compare_reduce_fusion), kind=kLoop, calls=%fused_computation.5 | loop fusion | flops 393216 | bytes 2097153 | tf_op jit(solution)/shard_map/add | solution.py:57
  110.7 0.0 reduce-scatter.2.cloned.1.call-update
  110.8 22.0 %reduce-scatter.2.cloned.1.call-done = f32[256,128]{1,0:T(8,128)} async-done(((f32[256,512]{1,0:T(8,128)}), f32[256,128]{1,0:T(8,128)}) %reduce-scatter.2.cloned.1.call-update) | async-done | bytes 131088 | tf_op jit(solution)/shard_map/reduce_scatter | solution.py:58
  (8 shorter events, 0.1 us)
Async XLA Ops:
  6.5 33.1 %all-gather.3.cloned.1.call-start = ((), (), s32[]{:S(2)}) async-start(), calls=%async_computation.1 | async-start | bytes 1310720 | tf_op jit(solution)/shard_map/all_gather | solution.py:23
  8.4 95.8 %all-reduce.2.cloned.1.call-start = ((), (), s32[]{:S(2)}) async-start(), calls=%async_computation.2 | async-start | bytes 524288 | tf_op jit(solution)/shard_map/psum | solution.py:34
  39.6 17.9 %collective-permute-start = (bf16[1024,512]{0,1:T(8,128)(2,1)}, bf16[1024,512]{0,1:T(8,128)(2,1)S(1)}, u32[]{:S(2)}, u32[]{:S(2)}) collective-permute-start(bf16[1024,512]{0,1:T(8,128)(2,1)} %all-gather.3.cloned.1.call-done), channel_id=1, source_target_pairs={{16,0},{17,1},{18,2},{19,3},{20,4},{21,5},{22,6},{23,7},{24,8},{25... | collective-permute-start | bytes 3145736 | tf_op jit(solution)/shard_map/ppermute | solution.py:10
  56.2 51.7 %collective-permute-start.1 = (bf16[256,512]{0,1:T(8,128)(2,1)S(1)}, bf16[256,512]{0,1:T(8,128)(2,1)S(1)}, u32[]{:S(2)}, u32[]{:S(2)}) collective-permute-start(bf16[256,512]{0,1:T(8,128)(2,1)S(1)} %all_gather.11), channel_id=1, source_target_pairs={{16,0},{17,1},{18,2},{19,3},{20,4},{21,5},{22,6},{23,7},{24,8},{25... | collective-permute-start | bytes 786440 | tf_op jit(solution)/shard_map/ppermute | solution.py:10
  57.6 2.3 %copy-start = (bf16[1024,512]{0,1:T(8,128)(2,1)S(1)}, bf16[1024,512]{0,1:T(8,128)(2,1)}, u32[]{:S(2)}) copy-start(bf16[1024,512]{0,1:T(8,128)(2,1)} %all-gather.3.cloned.1.call-done) | copy-start | bytes 3145732
  59.9 1.3 copy-start.2
  61.1 71.7 %reduce-scatter.2.cloned.1.call-start = ((), (), s32[]{:S(2)}) async-start(), calls=%async_computation.3 | async-start | bytes 655360 | tf_op jit(solution)/shard_map/reduce_scatter | solution.py:58
  105.8 2.8 %copy-start.1 = (f32[4,128,128]{1,2,0:T(8,128)S(1)}, f32[4,128,128]{1,2,0:T(8,128)}, u32[]{:S(2)}) copy-start(f32[4,128,128]{1,2,0:T(8,128)} %all-reduce.2.cloned.1.call-done) | copy-start | bytes 786436
  105.8 3.3 %collective-permute-start.2 = (f32[256,512]{1,0:T(8,128)S(1)}, f32[256,512]{1,0:T(8,128)S(1)}, u32[]{:S(2)}, u32[]{:S(2)}) collective-permute-start(f32[256,512]{1,0:T(8,128)S(1)} %slice.29), channel_id=1, source_target_pairs={{0,16},{1,17},{2,18},{3,19},{4,20},{5,21},{6,22},{7,23},{8,24},{9,... | collective-permute-start | bytes 1572872 | tf_op jit(solution)/shard_map/ppermute | solution.py:10
Sparse Core Ops, SparseCore 0:
  8.9 30.6 all-gather.2
  61.2 42.9 all-reduce.1
  110.9 21.8 reduce-scatter.1
where the time goes:
time: 140 us; the launch traced here: 139 us
  waiting for transfers between devices  87.1 us (62%)
  blocking collectives  23.5 us (17%)
  between operations  13.3 us (10%)
  other arithmetic  5.3 us (4%)
  starting transfers between devices  4.1 us (3%)
  local copies, waits for them, and re-layouts  3.35 us (2%)
  matrix products  2.71 us (2%)
    psum x1, waiting for transfers between devices, per_device(): gram = lax.psum(partial_gram, 'ind')  33.8 us
    all_gather x1, waiting for transfers between devices, per_device(): lax.all_gather(dosages, 'col', axis=1, tiled=True)  31.2 us
    reduce_scatter x1, waiting for transfers between devices, per_device(): lax.psum_scatter(combined, 'col', scatter_dimension=1, tiled=True)  22 us
    all_gather x1, blocking collectives, per_device(): lax.all_gather(annotations, 'col', axis=1, tiled=True)  14.4 us
    all_gather x1, blocking collectives, per_device(): window_ends = lax.all_gather(window_end, 'col', axis=0, tiled=True)  9.09 us
    ppermute x3, starting transfers between devices, from_behind(): return lax.ppermute(array, axis, pairs)  4.02 us
  transfers between devices with their start and end apart: 6, of which 3 were waited for; matrix products, arithmetic and copies ran while one was open for 6% of the time, Pallas kernels for 0%

commit v1 on v0

--- a/solution.py
+++ b/solution.py
@@ -18,7 +18,14 @@
     ann_rows = annotations.shape[0]
     group_width = band_count * tile_size
     sample_count = ind_rows * lax.axis_size("ind")
-    window_ends = lax.all_gather(window_end, "col", axis=0, tiled=True)
+    size = lax.axis_size("col")
+    right = [(i_2, (i_2 + 1) % size) for i_2 in range(size)]
+    pieces = [window_end]
+    for far in range(1, size):
+        pieces = [lax.ppermute(pieces[0], "col", right), *pieces]
+    out = jnp.concatenate(pieces, axis=0)
+    turn = (lax.axis_index("col") + 1) * pieces[-1].shape[0]
+    window_ends = jnp.roll(out, turn, axis=0)
     group_x, group_a = (
         lax.all_gather(dosages, "col", axis=1, tiled=True),
         lax.all_gather(annotations, "col", axis=1, tiled=True),

time: 140 us -> 134 us (0.957)
  blocking collectives: 23.5 us -> 16.2 us
  starting transfers between devices: 4.1 us -> 8 us
  waiting for transfers between devices: 87.1 us -> 84.5 us
    all_gather x1, waiting for transfers between devices: 31.2 us -> 11 us  [per_device(): lax.all_gather(dosages, 'col', axis=1, tiled=True)]
    ppermute x0 -> x3, waiting for transfers between devices: none -> 9.94 us  [per_device(): pieces = [lax.ppermute(pieces[0], 'col', right), *pieces]]
    all_gather x1 -> x0, blocking collectives: 9.09 us -> none  [per_device(): window_ends = lax.all_gather(window_end, 'col', axis=0, tiled=True)]
    psum x1, waiting for transfers between devices: 33.8 us -> 41.4 us  [per_device(): gram = lax.psum(partial_gram, 'ind')]
    ppermute x0 -> x3, starting transfers between devices: none -> 3.9 us  [per_device(): pieces = [lax.ppermute(pieces[0], 'col', right), *pieces]]
    all_gather x1, blocking collectives: 14.4 us -> 16.2 us  [per_device(): lax.all_gather(annotations, 'col', axis=1, tiled=True)]
    unnamed x8 -> x15, local copies, waits for them, and re-layouts: 2.74 us -> 2.81 us
  transfers between devices with their start and end apart: 6 -> 9, of which waited for: 3 -> 5; matrix products, arithmetic and copies ran while one was open for 6% -> 6% of each run, Pallas kernels for 0% -> 0%
where the time goes in v1:
time: 134 us; the launch traced here: 133 us
  waiting for transfers between devices  84.5 us (63%)
  blocking collectives  16.2 us (12%)
  between operations  13.3 us (10%)
  starting transfers between devices  8 us (6%)
  other arithmetic  5.3 us (4%)
  local copies, waits for them, and re-layouts  3.49 us (3%)
  matrix products  2.71 us (2%)
    psum x1, waiting for transfers between devices, per_device(): gram = lax.psum(partial_gram, 'ind')  41.4 us
    reduce_scatter x1, waiting for transfers between devices, per_device(): lax.psum_scatter(combined, 'col', scatter_dimension=1, tiled=True)  22 us
    all_gather x1, blocking collectives, per_device(): lax.all_gather(annotations, 'col', axis=1, tiled=True)  16.2 us
    all_gather x1, waiting for transfers between devices, per_device(): lax.all_gather(dosages, 'col', axis=1, tiled=True)  11 us
    ppermute x3, waiting for transfers between devices, per_device(): pieces = [lax.ppermute(pieces[0], 'col', right), *pieces]  9.94 us
    ppermute x3, starting transfers between devices, from_behind(): return lax.ppermute(array, axis, pairs)  4.02 us
    ppermute x3, starting transfers between devices, per_device(): pieces = [lax.ppermute(pieces[0], 'col', right), *pieces]  3.9 us
    unnamed x15, local copies, waits for them, and re-layouts  2.81 us
  transfers between devices with their start and end apart: 9, of which 5 were waited for; matrix products, arithmetic and copies ran while one was open for 6% of the time, Pallas kernels for 0%

profile of v1, /device:TPU:0, one launch (start us, length us, event | category | flops | bytes accessed | tf_op | source)
XLA Modules:
  0.0 133.5 jit_solution(1246180010778010427)
XLA Ops:
  6.5 1.8 %copy.8 = bf16[1024,128]{0,1:T(8,128)(2,1)} copy(bf16[1024,128]{1,0:T(8,128)(2,1)} %param.5) | data formatting | bytes 524288 | tf_op args[0]
  8.3 0.0 all-gather.2.cloned.1.call-update
  8.4 0.0 all-reduce.2.cloned.1.call-start
  8.4 3.1 %collective-permute-start = (s32[128]{0:T(128)}, s32[128]{0:T(128)S(1)}, u32[]{:S(2)}, u32[]{:S(2)}) collective-permute-start(s32[128]{0:T(128)} %param.7), channel_id=1, source_target_pairs={{0,4},{4,8},{8,12},{12,0},{1,5},{5,9},{9,13},{13,1},{2,6},{6,10},{... | collective-permute-start | bytes 1544 | tf_op jit(solution)/shard_map/ppermute | solution.py:25
  11.5 0.9 copy.10
  12.5 16.2 %all_gather.7 = bf16[256,512]{0,1:T(8,128)(2,1)S(1)} all-gather(bf16[256,128]{0,1:T(8,128)(2,1)S(1)} %copy.10), channel_id=1, replica_groups=mesh['row'=2,'col'=4,'ind'=4] {'col'}, dimensions={1}, use_global_device_ids=true | all-gather | bytes 327680 | tf_op jit(solution)/shard_map/all_gather | solution.py:31
  28.7 1.3 collective-permute-start.4
  30.0 11.0 %all-gather.2.cloned.1.call-done = bf16[1024,512]{0,1:T(8,128)(2,1)} async-done(((bf16[1024,128]{0,1:T(8,128)(2,1)}), bf16[1024,512]{0,1:T(8,128)(2,1)}) %all-gather.2.cloned.1.call-update) | async-done | bytes 1048592 | tf_op jit(solution)/shard_map/all_gather | solution.py:30
  41.0 1.3 collective-permute-start.3
  42.3 0.1 iota_add_fusion
  42.4 0.1 iota_add_fusion.1
  42.4 0.8 collective-permute-start.1
  43.2 4.6 %collective-permute-done.1 = s32[128]{0:T(128)S(1)} collective-permute-done((s32[128]{0:T(128)S(1)}, s32[128]{0:T(128)S(1)}, u32[]{:S(2)}, u32[]{:S(2)}) %collective-permute-start.1) | collective-permute-done | bytes 544 | tf_op jit(solution)/shard_map/ppermute | solution.py:25
  47.8 5.4 %collective-permute-done.2 = s32[128]{0:T(128)S(1)} collective-permute-done((s32[128]{0:T(128)S(1)}, s32[128]{0:T(128)S(1)}, u32[]{:S(2)}, u32[]{:S(2)}) %collective-permute-start.2) | collective-permute-done | bytes 544 | tf_op jit(solution)/shard_map/ppermute | solution.py:25
  53.3 2.3 %fusion = bf16[1024,512]{0,1:T(8,128)(2,1)S(1)} fusion(s32[]{:T(128)S(6)} %select_n.27, bf16[1024,512]{0,1:T(8,128)(2,1)} %all-gather.2.cloned.1.call-done, bf16[1024,512]{0,1:T(8,128)(2,1)S(1)} %collective-permute-done.3), kind=kLoop, calls=%fused_computation.3 | loop fusion | flops 2097152 | bytes 3145732 | tf_op jit(solution)/shard_map/concatenate | solution.py:34
  55.6 1.1 convolution_bitcast_fusion
  56.7 0.0 all-reduce.2.cloned.1.call-update
  56.7 0.0 reduce-scatter.2.cloned.1.call-start
  56.8 0.1 dynamic-slice_bitcast_fusion
  56.9 41.4 %all-reduce.2.cloned.1.call-done = f32[4,128,128]{1,2,0:T(8,128)} async-done(((f32[4,128,128]{1,2,0:T(8,128)}), f32[4,128,128]{1,2,0:T(8,128)}) %all-reduce.2.cloned.1.call-update) | async-done | bytes 262160 | tf_op jit(solution)/shard_map/psum | solution.py:41
  98.3 1.2 fusion.3
  99.6 0.2 copy.12
  99.8 0.1 broadcast_in_dim.11
  99.9 0.1 constant_dynamic-update-slice_fusion.8
  100.0 1.5 %collective-permute-start.5 = (f32[256,512]{1,0:T(8,128)S(1)}, f32[256,512]{1,0:T(8,128)S(1)}, u32[]{:S(2)}, u32[]{:S(2)}) collective-permute-start(f32[256,512]{1,0:T(8,128)S(1)} %slice.29), channel_id=1, source_target_pairs={{0,16},{1,17},{2,18},{3,19},{4,20},{5,21},{6,22},{7,23},{8,24},{9,... | collective-permute-start | bytes 1572872 | tf_op jit(solution)/shard_map/ppermute | solution.py:10
  101.5 0.6 compare_reduce_fusion
  102.1 0.6 fusion.2
  102.7 0.4 fusion.4
  103.1 0.2 copy.15
  103.3 1.6 %fusion.1 = f32[256,512]{1,0:T(8,128)} fusion(f32[256,512]{1,0:T(8,128)S(1)} %collective-permute-done.5, f32[256,512]{1,0:T(8,128)S(1)} %copy.15, f32[256,1024]{1,0:T(8,128)S(1)} %constant_dynamic-update-slice_fusion.8, pred[]{:T(512)} %compare_reduce_fusion), kind=kLoop, calls=%fused_computation.5 | loop fusion | flops 393216 | bytes 2097153 | tf_op jit(solution)/shard_map/add | solution.py:64
  104.9 0.0 reduce-scatter.2.cloned.1.call-update
  104.9 22.0 %reduce-scatter.2.cloned.1.call-done = f32[256,128]{1,0:T(8,128)} async-done(((f32[256,512]{1,0:T(8,128)}), f32[256,128]{1,0:T(8,128)}) %reduce-scatter.2.cloned.1.call-update) | async-done | bytes 131088 | tf_op jit(solution)/shard_map/reduce_scatter | solution.py:65
  (23 shorter events, 0.1 us)
Async XLA Ops:
  6.5 46.7 %copy-start.2 = (s32[128]{0:T(128)S(1)}, s32[128]{0:T(128)}, u32[]{:S(2)}) copy-start(s32[128]{0:T(128)} %param.7) | copy-start | bytes 1540
  6.5 34.5 %all-gather.2.cloned.1.call-start = ((), (), s32[]{:S(2)}) async-start(), calls=%async_computation.1 | async-start | bytes 1310720 | tf_op jit(solution)/shard_map/all_gather | solution.py:30
  8.4 90.0 %all-reduce.2.cloned.1.call-start = ((), (), s32[]{:S(2)}) async-start(), calls=%async_computation.2 | async-start | bytes 524288 | tf_op jit(solution)/shard_map/psum | solution.py:41
  8.4 34.0 %collective-permute-start = (s32[128]{0:T(128)}, s32[128]{0:T(128)S(1)}, u32[]{:S(2)}, u32[]{:S(2)}) collective-permute-start(s32[128]{0:T(128)} %param.7), channel_id=1, source_target_pairs={{0,4},{4,8},{8,12},{12,0},{1,5},{5,9},{9,13},{13,1},{2,6},{6,10},{... | collective-permute-start | bytes 1544 | tf_op jit(solution)/shard_map/ppermute | solution.py:25
  28.7 73.4 %collective-permute-start.4 = (bf16[256,512]{0,1:T(8,128)(2,1)S(1)}, bf16[256,512]{0,1:T(8,128)(2,1)S(1)}, u32[]{:S(2)}, u32[]{:S(2)}) collective-permute-start(bf16[256,512]{0,1:T(8,128)(2,1)S(1)} %all_gather.7), channel_id=1, source_target_pairs={{16,0},{17,1},{18,2},{19,3},{20,4},{21,5},{22,6},{23,7},{24,8},{25... | collective-permute-start | bytes 786440 | tf_op jit(solution)/shard_map/ppermute | solution.py:10
  41.0 12.3 %collective-permute-start.3 = (bf16[1024,512]{0,1:T(8,128)(2,1)}, bf16[1024,512]{0,1:T(8,128)(2,1)S(1)}, u32[]{:S(2)}, u32[]{:S(2)}) collective-permute-start(bf16[1024,512]{0,1:T(8,128)(2,1)} %all-gather.2.cloned.1.call-done), channel_id=1, source_target_pairs={{16,0},{17,1},{18,2},{19,3},{20,4},{21,5},{22,6},{23,7},{24,8},{25... | collective-permute-start | bytes 3145736 | tf_op jit(solution)/shard_map/ppermute | solution.py:10
  42.4 5.4 %collective-permute-start.1 = (s32[128]{0:T(128)S(1)}, s32[128]{0:T(128)S(1)}, u32[]{:S(2)}, u32[]{:S(2)}) collective-permute-start(s32[128]{0:T(128)S(1)} %collective-permute-done), channel_id=1, source_target_pairs={{0,4},{4,8},{8,12},{12,0},{1,5},{5,9},{9,13},{13,1},{2,6},{6,10},{... | collective-permute-start | bytes 1544 | tf_op jit(solution)/shard_map/ppermute | solution.py:25
  47.8 5.4 %collective-permute-start.2 = (s32[128]{0:T(128)S(1)}, s32[128]{0:T(128)S(1)}, u32[]{:S(2)}, u32[]{:S(2)}) collective-permute-start(s32[128]{0:T(128)S(1)} %collective-permute-done.1), channel_id=1, source_target_pairs={{0,4},{4,8},{8,12},{12,0},{1,5},{5,9},{9,13},{13,1},{2,6},{6,10},{... | collective-permute-start | bytes 1544 | tf_op jit(solution)/shard_map/ppermute | solution.py:25
  53.2 2.3 %copy-start = (bf16[1024,512]{0,1:T(8,128)(2,1)S(1)}, bf16[1024,512]{0,1:T(8,128)(2,1)}, u32[]{:S(2)}) copy-start(bf16[1024,512]{0,1:T(8,128)(2,1)} %all-gather.2.cloned.1.call-done) | copy-start | bytes 3145732
  56.7 70.2 %reduce-scatter.2.cloned.1.call-start = ((), (), s32[]{:S(2)}) async-start(), calls=%async_computation.3 | async-start | bytes 655360 | tf_op jit(solution)/shard_map/reduce_scatter | solution.py:65
  99.9 2.8 %copy-start.1 = (f32[4,128,128]{1,2,0:T(8,128)S(1)}, f32[4,128,128]{1,2,0:T(8,128)}, u32[]{:S(2)}) copy-start(f32[4,128,128]{1,2,0:T(8,128)} %all-reduce.2.cloned.1.call-done) | copy-start | bytes 786436
  100.0 3.3 %collective-permute-start.5 = (f32[256,512]{1,0:T(8,128)S(1)}, f32[256,512]{1,0:T(8,128)S(1)}, u32[]{:S(2)}, u32[]{:S(2)}) collective-permute-start(f32[256,512]{1,0:T(8,128)S(1)} %slice.29), channel_id=1, source_target_pairs={{0,16},{1,17},{2,18},{3,19},{4,20},{5,21},{6,22},{7,23},{8,24},{9,... | collective-permute-start | bytes 1572872 | tf_op jit(solution)/shard_map/ppermute | solution.py:10
Sparse Core Ops, SparseCore 0:
  8.9 32.0 all-gather.1
  56.9 41.4 all-reduce.1
  105.1 21.8 reduce-scatter.1
